TPU v7x, 32 devices: a whole 2x2x4 slice. The times are simulated.
32 devices in a mesh: groups: 1, dev: 8 (over z, y), side: 4 (over x, core).
Axes of the slice: x: 2, y: 2, z: 4, core: 2. Of those that a mesh axis runs over, the one named last changes fastest.
Arguments:
- queries: bfloat16 [256, 4096], P(('groups', 'dev', 'side')), may hold values from -160 to 160
- kv_cache: bfloat16 [256, 192, 1024], P(('groups', 'dev', 'side')), may hold values from -4 to 4
- new_kv: bfloat16 [256, 1024], P(('groups', 'dev', 'side')), may hold values from -4 to 4
- lengths: int32 [256], P(('groups', 'dev', 'side')), may hold values from 24 to 192, as said below
- residual: bfloat16 [256, 2048], P(('groups', 'dev', 'side')), may hold values from -36 to 36
- w_out: bfloat16 [4096, 2048], P('side'), may hold values from -0.59765625 to 0.59765625
- norm_gain: float32 [2048], replicated, may hold values from 0.5 to 1.5
- expert_ids: int32 [256, 8], P(('groups', 'dev', 'side')), may hold values from 0 to 15, all different within a row; in each aligned block of 8 rows (0 to 7, 8 to 15, ...) at most 8 rows name the same one
- route_level: int32 [256, 8], P(('groups', 'dev', 'side')), may hold values from 1 to 255
- w_in: bfloat16 [32, 2048, 768], P(('dev', 'side')), may hold values from -0.125 to 0.125
- w_down: bfloat16 [32, 384, 2048], P(('dev', 'side')), may hold values from -0.4375 to 0.4375
Outputs:
- stream: bfloat16 [256, 2048], P(('groups', 'dev', 'side'))
- expert_sum: bfloat16 [256, 2048], P(('groups', 'dev', 'side'))
Inputs may be any that keep to these rules, and one draw needn't show every extreme that they name: `lengths`: in each aligned block of 8 requests some request has 192 cached tokens. `expert_ids`: A row names 8 different experts. In each aligned block of 8 rows no expert is named by more than 8 rows, and in some block some expert is named by exactly 8 rows.
All inputs are finite; a program needn't handle non-finite values.
Results may differ from a plain program's by a relative error of at most 0.013.
Values may be sent and summed in bfloat16 or wider, within the bound.
No kernel may reach another device: no remote copies, remote signals or barrier semaphores. Data moves between devices by JAX's collectives and lax.ppermute only.
A program may use at most 64 MiB of HBM per device.

v0:
```python
import math
import jax
import jax.numpy as jnp
from jax import lax
from jax.sharding import PartitionSpec as P

HQ = 32
KVH = 4
HD = 128
CACHE = 192


def partner(block, axis, bit):
    count = lax.axis_size(axis)
    route = []
    for low in range(count):
        high = low | 1 << bit
        if high != low and high < count:
            route += [(low, high), (high, low)]
    return lax.ppermute(block, axis, route)


def attend(queries, kv_cache, new_kv, lengths):
    req_rows = queries.shape[0]
    group_size = HQ // KVH
    split_at = KVH * HD
    grouped_q = queries.reshape(req_rows, KVH, group_size, HD)
    key_rows = kv_cache[:, :, :split_at].reshape(req_rows, CACHE, KVH, HD)
    value_rows = kv_cache[:, :, split_at:].reshape(req_rows, CACHE, KVH, HD)
    new_key = new_kv[:, :split_at].reshape(req_rows, KVH, HD)
    new_value = new_kv[:, split_at:].reshape(req_rows, KVH, HD)
    scaling = 1.0 / math.sqrt(HD)
    scores = (
        jnp.einsum("rgqd,rlgd->rgql", grouped_q, key_rows, preferred_element_type=jnp.float32)
        * scaling
    )
    own_score = (
        jnp.einsum("rgqd,rgd->rgq", grouped_q, new_key, preferred_element_type=jnp.float32)
        * scaling
    )
    visible = (jnp.arange(CACHE)[None, :] < lengths[:, None])[:, None, None, :]
    scores = jnp.where(visible, scores, -jnp.inf)
    peak = jnp.maximum(jnp.max(scores, axis=3), own_score)
    weights = jnp.where(visible, jnp.exp(scores - peak[..., None]), 0.0)
    own_weight = jnp.exp(own_score - peak)
    denominator = jnp.sum(weights, axis=3) + own_weight
    probability = (weights / denominator[..., None]).astype(jnp.bfloat16)
    own_prob = (own_weight / denominator).astype(jnp.bfloat16)
    mixed = jnp.einsum(
        "rgql,rlgd->rgqd", probability, value_rows, preferred_element_type=jnp.float32
    )
    mixed = (
        mixed
        + own_prob.astype(jnp.float32)[..., None] * new_value.astype(jnp.float32)[:, :, None, :]
    )
    return mixed.reshape(req_rows, HQ * HD).astype(jnp.bfloat16)


def expert_rows(received, gate_up_w, down_w):
    model_width = received.shape[2]
    flattened = received.reshape(-1, model_width)
    half_units = down_w.shape[0]
    gate_up = jnp.dot(flattened, gate_up_w, preferred_element_type=jnp.float32)
    hidden = (jax.nn.silu(gate_up[:, :half_units]) * gate_up[:, half_units:]).astype(jnp.bfloat16)
    result = jnp.dot(hidden, down_w, preferred_element_type=jnp.float32)
    return result.reshape(received.shape[0], received.shape[1], model_width)


def body(
    queries,
    kv_cache,
    new_kv,
    lengths,
    residual,
    w_out,
    norm_gain,
    expert_ids,
    route_level,
    w_in,
    w_down,
):
    req_rows = queries.shape[0]
    top_count = expert_ids.shape[1]
    model_width = residual.shape[1]
    attended = attend(queries, kv_cache, new_kv, lengths)
    columns = lax.all_to_all(attended, "side", split_axis=1, concat_axis=0, tiled=True)
    attention = lax.psum_scatter(
        jnp.dot(columns, w_out, preferred_element_type=jnp.float32),
        "side",
        scatter_dimension=0,
        tiled=True,
    )
    stream = residual.astype(jnp.float32) + attention
    mean_square = jnp.mean(stream * stream, axis=1, keepdims=True)
    normed = (stream * lax.rsqrt(mean_square + 1e-06) * norm_gain[None, :]).astype(jnp.bfloat16)
    shares = route_level.astype(jnp.float32)
    shares = shares / jnp.sum(shares, axis=1, keepdims=True)
    shards = lax.axis_size("dev") * lax.axis_size("side")
    experts = shards // 2
    capacity = 2 * req_rows * top_count // experts
    pair_expert = expert_ids.reshape(-1)
    one_hot = (pair_expert[:, None] == jnp.arange(experts, dtype=jnp.int32)[None, :]).astype(
        jnp.int32
    )
    slot_rank = jnp.sum((jnp.cumsum(one_hot, axis=0) - 1) * one_hot, axis=1)
    target = pair_expert * capacity + slot_rank
    placed = target[None, :] == jnp.arange(experts * capacity, dtype=jnp.int32)[:, None]
    placed = placed.reshape(experts * capacity, req_rows, top_count)
    picker = jnp.any(placed, axis=2).astype(jnp.bfloat16)
    mixing = jnp.sum(jnp.where(placed, shares[None, :, :], 0.0), axis=2).T
    outbox = jnp.dot(picker, normed, preferred_element_type=jnp.float32).astype(jnp.bfloat16)
    grouped = outbox.reshape(experts, capacity, model_width)
    pair_side = lax.axis_index("side") % 2
    gate_up_w = w_in[0]
    down_w = w_down[0]
    doubled = jnp.broadcast_to(grouped[:, None], (experts, 2, capacity, model_width))
    doubled = doubled.reshape(shards, capacity, model_width)
    partials = expert_rows(
        lax.all_to_all(doubled, ("dev", "side"), split_axis=0, concat_axis=0, tiled=True),
        gate_up_w,
        down_w,
    )
    halved = partials.reshape(shards, 2, capacity // 2, model_width)
    retained = jnp.where(pair_side == 0, halved[:, 0], halved[:, 1])
    handed = jnp.where(pair_side == 0, halved[:, 1], halved[:, 0])
    gained = partner(handed, "side", 0)
    joined = (retained + gained).astype(jnp.bfloat16)
    returned = lax.all_to_all(joined, ("dev", "side"), split_axis=0, concat_axis=0, tiled=True)
    outputs = returned.reshape(experts, capacity, model_width)
    expert_sum = jnp.dot(
        mixing,
        outputs.reshape(experts * capacity, model_width).astype(jnp.float32),
        precision=lax.Precision.HIGHEST,
    )
    return (stream.astype(jnp.bfloat16), expert_sum.astype(jnp.bfloat16))


def solution(mesh):
    return jax.shard_map(
        body,
        mesh=mesh,
        in_specs=(
            P(("groups", "dev", "side"), None),
            P(("groups", "dev", "side"), None, None),
            P(("groups", "dev", "side"), None),
            P(("groups", "dev", "side")),
            P(("groups", "dev", "side"), None),
            P("side", None),
            P(),
            P(("groups", "dev", "side"), None),
            P(("groups", "dev", "side"), None),
            P(("dev", "side"), None, None),
            P(("dev", "side"), None, None),
        ),
        out_specs=(P(("groups", "dev", "side"), None), P(("groups", "dev", "side"), None)),
        check_vma=False,
    )
```

profile of v0, /device:TPU:0, one launch (start us, length us, event | category | flops | bytes accessed | tf_op | source)
XLA Modules:
  0.0 121.0 jit_solution(14539800376660734263)
XLA Ops:
  7.2 0.0 copy-start
  7.2 0.9 iota_compare_fusion.2
  8.1 0.8 bitcast_convert_fusion
  8.9 2.5 %slice_bitcast_fusion.1 = (bf16[8,24,4,8,128]{4,3,2,1,0:T(8,128)(2,1)S(1)}, bf16[8,24,4,8,128]{4,3,2,1,0:T(8,128)(2,1)S(1)}) fusion(bf16[8,192,1024]{2,1,0:T(8,128)(2,1)} %param.12), kind=kLoop, calls=%fused_computation.14 | loop fusion | bytes 6291456
  11.3 0.0 copy-done.2
  11.3 0.2 fusion.34
  11.5 1.0 fusion.46
  12.5 0.2 fusion.26
  12.8 0.0 copy-start.3
  12.8 0.6 fusion.20
  13.4 0.6 copy.34
  14.0 4.2 %all-to-all-start = ((bf16[8,4,1024]{2,0,1:T(8,128)(2,1)}), bf16[8,4,1024]{2,0,1:T(8,128)(2,1)S(1)}, u32[]{:S(2)}, u32[]{:S(2)}) async-start(bf16[8,4,1024]{2,0,1:T(8,128)(2,1)} %copy.34), calls=%async_computation | async-start | bytes 131072 | tf_op jit(solution)/shard_map/all_to_all | solution.py:86
  18.3 0.0 reduce-scatter.2.cloned.1.call-start
  18.3 0.0 copy-done.3
  18.3 0.1 eq.35
  18.4 4.0 %all-to-all-done = bf16[8,4,1024]{2,0,1:T(8,128)(2,1)S(1)} async-done(((bf16[8,4,1024]{2,0,1:T(8,128)(2,1)}), bf16[8,4,1024]{2,0,1:T(8,128)(2,1)S(1)}, u32[]{:S(2)}, u32[]{:S(2)}) %all-to-all-start) | async-done | bytes 65568 | tf_op jit(solution)/shard_map/all_to_all | solution.py:86
  22.4 3.7 %fusion.32 = f32[32,2048]{1,0:T(8,128)} fusion(bf16[1024,2048]{1,0:T(8,128)(2,1)} %param.16, bf16[8,4,1024]{2,0,1:T(8,128)(2,1)S(1)} %all-to-all-done), kind=kOutput, calls=%fused_computation.33 | convolution fusion | flops 134217728 | bytes 4521984 | tf_op jit(solution)/shard_map/dot_general | solution.py:88
  26.1 0.0 reduce-scatter.2.cloned.1.call-update
  26.1 0.1 fusion.40
  26.2 0.1 reduce_window_sum.11
  26.3 0.2 select_reduce_fusion.1
  26.5 0.1 reduce_sum.49
  26.6 0.1 fusion.39
  26.7 20.5 %reduce-scatter.2.cloned.1.call-done = f32[8,2048]{1,0:T(8,128)} async-done(((f32[32,2048]{1,0:T(8,128)}), f32[8,2048]{1,0:T(8,128)}) %reduce-scatter.2.cloned.1.call-update) | async-done | bytes 65552 | tf_op jit(solution)/shard_map/reduce_scatter | solution.py:87
  47.2 0.0 copy-done.1
  47.2 1.6 %multiply_reduce_fusion = (f32[8]{0:T(128)S(1)}, bf16[8,2048]{1,0:T(8,128)(2,1)}) fusion(f32[8,2048]{1,0:T(8,128)} %reduce-scatter.2.cloned.1.call-done, bf16[8,2048]{1,0:T(8,128)(2,1)S(1)} %copy-done.1), kind=kLoop, calls=%fused_computation.36 | loop fusion | flops 81912 | bytes 131104 | tf_op jit(solution)/shard_map/reduce_sum | solution.py:94
  48.8 0.0 copy-done.5
  48.8 1.2 fusion.2
  50.0 1.2 broadcast_in_dim.57
  51.2 4.7 %all-to-all-start.1 = ((bf16[32,8,2048]{2,1,0:T(8,128)(2,1)}), bf16[32,8,2048]{2,1,0:T(8,128)(2,1)}, u32[]{:S(2)}, u32[]{:S(2)}) async-start(bf16[32,8,2048]{2,1,0:T(8,128)(2,1)} %bitcast.63), calls=%async_computation.2 | async-start | bytes 2097152 | tf_op jit(solution)/shard_map/all_to_all | solution.py:119
  55.9 26.2 %all-to-all-done.1 = bf16[32,8,2048]{2,1,0:T(8,128)(2,1)} async-done(((bf16[32,8,2048]{2,1,0:T(8,128)(2,1)}), bf16[32,8,2048]{2,1,0:T(8,128)(2,1)}, u32[]{:S(2)}, u32[]{:S(2)}) %all-to-all-start.1) | async-done | bytes 1048608 | tf_op jit(solution)/shard_map/all_to_all | solution.py:119
  82.1 2.2 %fusion = f32[256,768]{1,0:T(8,128)S(1)} fusion(bf16[1,2048,768]{2,1,0:T(8,128)(2,1)S(1)} %copy-done, bf16[32,8,2048]{2,1,0:T(8,128)(2,1)} %all-to-all-done.1), kind=kOutput, calls=%fused_computation | convolution fusion | flops 805306368 | bytes 4980736 | tf_op jit(solution)/shard_map/dot_general | solution.py:63
  84.3 0.1 fusion.25
  84.4 0.1 dot_general.32
  84.5 2.1 %fusion.9 = f32[32,2,4,2048]{3,0,2,1:T(8,128)S(1)} fusion(bf16[1,384,2048]{2,1,0:T(8,128)(2,1)} %param.21, bf16[32,2,4,384]{3,2,1,0:T(4,128)(2,1)S(1)} %dot_general.32), kind=kOutput, calls=%fused_computation.11 | convolution fusion | flops 402653184 | bytes 3866624 | tf_op jit(solution)/shard_map/dot_general | solution.py:65
  86.6 0.1 select_bitcast_fusion
  86.7 0.1 collective-permute-start
  86.8 2.6 %collective-permute-done = f32[32,4,2048]{2,0,1:T(8,128)S(1)} collective-permute-done((f32[32,4,2048]{2,0,1:T(8,128)S(1)}, f32[32,4,2048]{2,0,1:T(8,128)S(1)}, u32[]{:S(2)}, u32[]{:S(2)}) %collective-permute-start) | collective-permute-done | bytes 1048608 | tf_op jit(solution)/shard_map/ppermute | solution.py:20
  89.5 0.2 fusion.23
  89.6 0.0 copy-start.4
  89.7 1.2 %copy.36 = bf16[32,4,2048]{2,1,0:T(4,128)(2,1)} copy(bf16[32,4,2048]{2,0,1:T(8,128)(2,1)S(1)} %fusion.23) | data formatting | bytes 1048576 | tf_op jit(solution)/shard_map/convert_element_type | solution.py:127
  90.9 3.7 %all-to-all-start.2 = ((bf16[32,4,2048]{2,1,0:T(4,128)(2,1)}), bf16[32,4,2048]{2,1,0:T(4,128)(2,1)}, u32[]{:S(2)}, u32[]{:S(2)}) async-start(bf16[32,4,2048]{2,1,0:T(4,128)(2,1)} %copy.36), calls=%async_computation.3 | async-start | bytes 1048576 | tf_op jit(solution)/shard_map/all_to_all | solution.py:128
  94.6 0.1 convert_reduce_fusion
  94.8 0.1 convert_divide_fusion
  94.8 0.1 select_reduce_fusion
  94.9 15.3 %all-to-all-done.2 = bf16[32,4,2048]{2,1,0:T(4,128)(2,1)} async-done(((bf16[32,4,2048]{2,1,0:T(4,128)(2,1)}), bf16[32,4,2048]{2,1,0:T(4,128)(2,1)}, u32[]{:S(2)}, u32[]{:S(2)}) %all-to-all-start.2) | async-done | bytes 524320 | tf_op jit(solution)/shard_map/all_to_all | solution.py:128
  110.2 2.0 %reshape_reshape.4 = bf16[128,2048]{1,0:T(8,128)(2,1)} reshape(bf16[32,4,2048]{2,1,0:T(4,128)(2,1)} %all-to-all-done.2) | data formatting | bytes 1048576 | tf_op jit(solution)/shard_map/reshape;reshape | solution.py:132
  112.2 2.0 %convolution_convert_fusion.1 = bf16[8,2048]{1,0:T(8,128)(2,1)} fusion(f32[128,8]{0,1:T(8,128)S(1)} %select_reduce_fusion, bf16[128,2048]{1,0:T(8,128)(2,1)} %reshape_reshape.4), kind=kOutput, calls=%fused_computation.4 | convolution fusion | flops 25182208 | bytes 561152 | tf_op jit(solution)/shard_map/dot_general | solution.py:130
  (11 shorter events, 0.1 us)
Async XLA Ops:
  7.2 74.9 %copy-start = (bf16[1,2048,768]{2,1,0:T(8,128)(2,1)S(1)}, bf16[1,2048,768]{2,1,0:T(8,128)(2,1)}, u32[]{:S(2)}) copy-start(bf16[1,2048,768]{2,1,0:T(8,128)(2,1)} %param.20) | copy-start | bytes 9437188
  8.9 2.5 %copy-start.2 = (bf16[8,4096]{1,0:T(8,128)(2,1)S(1)}, bf16[8,4096]{1,0:T(8,128)(2,1)}, u32[]{:S(2)}) copy-start(bf16[8,4096]{1,0:T(8,128)(2,1)} %param.11) | copy-start | bytes 196612
  12.8 5.5 %copy-start.3 = (s32[8,8]{1,0:T(8,128)S(1)}, s32[8,8]{1,0:T(8,128)}, u32[]{:S(2)}) copy-start(s32[8,8]{1,0:T(8,128)} %param.18) | copy-start | bytes 772
  14.0 8.4 %all-to-all-start = ((bf16[8,4,1024]{2,0,1:T(8,128)(2,1)}), bf16[8,4,1024]{2,0,1:T(8,128)(2,1)S(1)}, u32[]{:S(2)}, u32[]{:S(2)}) async-start(bf16[8,4,1024]{2,0,1:T(8,128)(2,1)} %copy.34), calls=%async_computation | async-start | bytes 131072 | tf_op jit(solution)/shard_map/all_to_all | solution.py:86
  18.3 28.9 %reduce-scatter.2.cloned.1.call-start = ((), (), s32[]{:S(2)}) async-start(), calls=%async_computation.4 | async-start | bytes 327680 | tf_op jit(solution)/shard_map/reduce_scatter | solution.py:87
  18.4 28.8 %copy-start.1 = (bf16[8,2048]{1,0:T(8,128)(2,1)S(1)}, bf16[8,2048]{1,0:T(8,128)(2,1)}, u32[]{:S(2)}) copy-start(bf16[8,2048]{1,0:T(8,128)(2,1)} %param.15) | copy-start | bytes 98308
  18.4 30.4 %copy-start.5 = (f32[2048]{0:T(1024)S(1)}, f32[2048]{0:T(1024)}, u32[]{:S(2)}) copy-start(f32[2048]{0:T(1024)} %param.17) | copy-start | bytes 24580
  51.2 30.9 %all-to-all-start.1 = ((bf16[32,8,2048]{2,1,0:T(8,128)(2,1)}), bf16[32,8,2048]{2,1,0:T(8,128)(2,1)}, u32[]{:S(2)}, u32[]{:S(2)}) async-start(bf16[32,8,2048]{2,1,0:T(8,128)(2,1)} %bitcast.63), calls=%async_computation.2 | async-start | bytes 2097152 | tf_op jit(solution)/shard_map/all_to_all | solution.py:119
  86.7 2.7 %collective-permute-start = (f32[32,4,2048]{2,0,1:T(8,128)S(1)}, f32[32,4,2048]{2,0,1:T(8,128)S(1)}, u32[]{:S(2)}, u32[]{:S(2)}) collective-permute-start(f32[32,4,2048]{2,0,1:T(8,128)S(1)} %select_bitcast_fusion), channel_id=1, source_target_pairs={{0,1},{1,0},{2,3},{3,2},{4,5},{5,4},{6,7},{7,6},{8,9},{9,8},{10,11... | collective-permute-start | bytes 3145736 | tf_op jit(solution)/shard_map/ppermute | solution.py:20
  89.6 5.0 %copy-start.4 = (s32[8,8]{1,0:T(8,128)S(1)}, s32[8,8]{1,0:T(8,128)}, u32[]{:S(2)}) copy-start(s32[8,8]{1,0:T(8,128)} %param.19) | copy-start | bytes 772
  90.9 19.3 %all-to-all-start.2 = ((bf16[32,4,2048]{2,1,0:T(4,128)(2,1)}), bf16[32,4,2048]{2,1,0:T(4,128)(2,1)}, u32[]{:S(2)}, u32[]{:S(2)}) async-start(bf16[32,4,2048]{2,1,0:T(4,128)(2,1)} %copy.36), calls=%async_computation.3 | async-start | bytes 1048576 | tf_op jit(solution)/shard_map/all_to_all | solution.py:128
Sparse Core Ops, SparseCore 0:
  26.3 20.8 reduce-scatter.1
where the time goes:
time: 122 us; the launch traced here: 121 us
  waiting for transfers between devices  68.7 us (56%)
  between operations  14.2 us (12%)
  matrix products  12.9 us (11%)
  starting transfers between devices  12.8 us (10%)
  local copies, waits for them, and re-layouts  7.73 us (6%)
  other arithmetic  4.69 us (4%)
    all_to_all x1, waiting for transfers between devices, body(): lax.all_to_all(doubled, ('dev', 'side'), split_axis=0, concat_axis=0, til...  26.2 us
    reduce_scatter x1, waiting for transfers between devices, body(): lax.psum_scatter(jnp.dot(columns, w_out, preferred_element_type=jnp.float...  20.5 us
    all_to_all x1, waiting for transfers between devices, body(): lax.all_to_all(joined, ('dev', 'side'), split_axis=0, concat_axis=0, tile...  15.3 us
    all_to_all x1, starting transfers between devices, body(): lax.all_to_all(doubled, ('dev', 'side'), split_axis=0, concat_axis=0, til...  4.73 us
    all_to_all x1, starting transfers between devices, body(): lax.all_to_all(attended, 'side', split_axis=1, concat_axis=0, tiled=True)  4.24 us
    all_to_all x1, waiting for transfers between devices, body(): lax.all_to_all(attended, 'side', split_axis=1, concat_axis=0, tiled=True)  4.03 us
    all_to_all x1, starting transfers between devices, body(): lax.all_to_all(joined, ('dev', 'side'), split_axis=0, concat_axis=0, tile...  3.75 us
    dot_general x1, matrix products, body(): jnp.dot(columns, w_out, preferred_element_type=jnp.float32)  3.71 us
  transfers between devices with their start and end apart: 5, of which 5 were waited for; matrix products, arithmetic and copies ran while one was open for 1% of the time, Pallas kernels for 0%

commit v1 on v0

--- a/solution.py
+++ b/solution.py
@@ -83,7 +83,10 @@
     top_count = expert_ids.shape[1]
     model_width = residual.shape[1]
     attended = attend(queries, kv_cache, new_kv, lengths)
-    columns = lax.all_to_all(attended, "side", split_axis=1, concat_axis=0, tiled=True)
+    found_now = lax.axis_size("side")
+    newest = jnp.stack(jnp.split(attended, found_now, 1), 0)
+    y_new = lax.all_to_all(newest, "side", 0, 0)
+    columns = jnp.concatenate(y_new, 0)
     attention = lax.psum_scatter(
         jnp.dot(columns, w_out, preferred_element_type=jnp.float32),
         "side",

time: 122 us -> 122 us (level)
    unnamed x13 -> x14, local copies, waits for them, and re-layouts: 2.49 us -> 2.52 us
where the time goes in v1:
time: 122 us; the launch traced here: 121 us
  waiting for transfers between devices  68.7 us (56%)
  between operations  14.2 us (12%)
  matrix products  12.9 us (11%)
  starting transfers between devices  12.8 us (10%)
  local copies, waits for them, and re-layouts  7.1 us (6%)
  other arithmetic  5.32 us (4%)
    all_to_all x1, waiting for transfers between devices, body(): lax.all_to_all(doubled, ('dev', 'side'), split_axis=0, concat_axis=0, til...  26.2 us
    reduce_scatter x1, waiting for transfers between devices, body(): lax.psum_scatter(jnp.dot(columns, w_out, preferred_element_type=jnp.float...  20.5 us
    all_to_all x1, waiting for transfers between devices, body(): lax.all_to_all(joined, ('dev', 'side'), split_axis=0, concat_axis=0, tile...  15.3 us
    all_to_all x1, starting transfers between devices, body(): lax.all_to_all(doubled, ('dev', 'side'), split_axis=0, concat_axis=0, til...  4.73 us
    all_to_all x1, starting transfers between devices, body(): y_new = lax.all_to_all(newest, 'side', 0, 0)  4.24 us
    all_to_all x1, waiting for transfers between devices, body(): y_new = lax.all_to_all(newest, 'side', 0, 0)  4.03 us
    all_to_all x1, starting transfers between devices, body(): lax.all_to_all(joined, ('dev', 'side'), split_axis=0, concat_axis=0, tile...  3.75 us
    dot_general x1, matrix products, body(): jnp.dot(columns, w_out, preferred_element_type=jnp.float32)  3.71 us
  transfers between devices with their start and end apart: 5, of which 5 were waited for; matrix products, arithmetic and copies ran while one was open for 1% of the time, Pallas kernels for 0%

profile of v1, /device:TPU:0, one launch (start us, length us, event | category | flops | bytes accessed | tf_op | source)
XLA Modules:
  0.0 121.0 jit_solution(16230861676966407993)
XLA Ops:
  7.2 0.0 copy-start
  7.2 0.9 iota_compare_fusion.2
  8.1 0.8 bitcast_convert_fusion
  8.9 2.5 %slice_bitcast_fusion.1 = (bf16[8,24,4,8,128]{4,3,2,1,0:T(8,128)(2,1)S(1)}, bf16[8,24,4,8,128]{4,3,2,1,0:T(8,128)(2,1)S(1)}) fusion(bf16[8,192,1024]{2,1,0:T(8,128)(2,1)} %param.12), kind=kLoop, calls=%fused_computation.14 | loop fusion | bytes 6291456
  11.3 0.0 copy-done.2
  11.3 0.2 fusion.37
  11.5 1.0 fusion.49
  12.5 0.2 fusion.29
  12.8 0.0 copy-start.3
  12.8 0.6 fusion.23
  13.4 0.6 pad_maximum_fusion
  14.1 4.2 %all-to-all-start = ((bf16[4,8,1024]{2,1,0:T(8,128)(2,1)}), bf16[4,8,1024]{2,1,0:T(8,128)(2,1)S(1)}, u32[]{:S(2)}, u32[]{:S(2)}) async-start(bf16[4,8,1024]{2,1,0:T(8,128)(2,1)} %pad_maximum_fusion), calls=%async_computation | async-start | bytes 131072 | tf_op jit(solution)/shard_map/all_to_all | solution.py:88
  18.3 0.0 reduce-scatter.2.cloned.1.call-start
  18.3 0.0 copy-done.3
  18.3 0.1 eq.35
  18.4 4.0 %all-to-all-done = bf16[4,8,1024]{2,1,0:T(8,128)(2,1)S(1)} async-done(((bf16[4,8,1024]{2,1,0:T(8,128)(2,1)}), bf16[4,8,1024]{2,1,0:T(8,128)(2,1)S(1)}, u32[]{:S(2)}, u32[]{:S(2)}) %all-to-all-start) | async-done | bytes 65568 | tf_op jit(solution)/shard_map/all_to_all | solution.py:88
  22.4 3.7 %fusion.35 = f32[32,2048]{1,0:T(8,128)} fusion(bf16[1024,2048]{1,0:T(8,128)(2,1)} %param.16, bf16[4,8,1024]{2,1,0:T(8,128)(2,1)S(1)} %all-to-all-done), kind=kOutput, calls=%fused_computation.36 | convolution fusion | flops 134217728 | bytes 4521984 | tf_op jit(solution)/shard_map/dot_general | solution.py:91
  26.1 0.0 reduce-scatter.2.cloned.1.call-update
  26.1 0.1 fusion.43
  26.2 0.1 reduce_window_sum.11
  26.3 0.2 select_reduce_fusion.1
  26.5 0.1 reduce_sum.49
  26.6 0.1 fusion.42
  26.7 20.5 %reduce-scatter.2.cloned.1.call-done = f32[8,2048]{1,0:T(8,128)} async-done(((f32[32,2048]{1,0:T(8,128)}), f32[8,2048]{1,0:T(8,128)}) %reduce-scatter.2.cloned.1.call-update) | async-done | bytes 65552 | tf_op jit(solution)/shard_map/reduce_scatter | solution.py:90
  47.2 0.0 copy-done.1
  47.2 1.6 %multiply_reduce_fusion = (f32[8]{0:T(128)S(1)}, bf16[8,2048]{1,0:T(8,128)(2,1)}) fusion(f32[8,2048]{1,0:T(8,128)} %reduce-scatter.2.cloned.1.call-done, bf16[8,2048]{1,0:T(8,128)(2,1)S(1)} %copy-done.1), kind=kLoop, calls=%fused_computation.39 | loop fusion | flops 81912 | bytes 131104 | tf_op jit(solution)/shard_map/reduce_sum | solution.py:97
  48.8 0.0 copy-done.5
  48.8 1.2 fusion.2
  50.0 1.2 broadcast_in_dim.57
  51.2 4.7 %all-to-all-start.1 = ((bf16[32,8,2048]{2,1,0:T(8,128)(2,1)}), bf16[32,8,2048]{2,1,0:T(8,128)(2,1)}, u32[]{:S(2)}, u32[]{:S(2)}) async-start(bf16[32,8,2048]{2,1,0:T(8,128)(2,1)} %bitcast.75), calls=%async_computation.2 | async-start | bytes 2097152 | tf_op jit(solution)/shard_map/all_to_all | solution.py:122
  55.9 26.2 %all-to-all-done.1 = bf16[32,8,2048]{2,1,0:T(8,128)(2,1)} async-done(((bf16[32,8,2048]{2,1,0:T(8,128)(2,1)}), bf16[32,8,2048]{2,1,0:T(8,128)(2,1)}, u32[]{:S(2)}, u32[]{:S(2)}) %all-to-all-start.1) | async-done | bytes 1048608 | tf_op jit(solution)/shard_map/all_to_all | solution.py:122
  82.1 2.2 %fusion = f32[256,768]{1,0:T(8,128)S(1)} fusion(bf16[1,2048,768]{2,1,0:T(8,128)(2,1)S(1)} %copy-done, bf16[32,8,2048]{2,1,0:T(8,128)(2,1)} %all-to-all-done.1), kind=kOutput, calls=%fused_computation | convolution fusion | flops 805306368 | bytes 4980736 | tf_op jit(solution)/shard_map/dot_general | solution.py:63
  84.3 0.1 fusion.28
  84.4 0.1 dot_general.32
  84.5 2.1 %fusion.9 = f32[32,2,4,2048]{3,0,2,1:T(8,128)S(1)} fusion(bf16[1,384,2048]{2,1,0:T(8,128)(2,1)} %param.21, bf16[32,2,4,384]{3,2,1,0:T(4,128)(2,1)S(1)} %dot_general.32), kind=kOutput, calls=%fused_computation.11 | convolution fusion | flops 402653184 | bytes 3866624 | tf_op jit(solution)/shard_map/dot_general | solution.py:65
  86.6 0.1 select_bitcast_fusion
  86.7 0.1 collective-permute-start
  86.8 2.6 %collective-permute-done = f32[32,4,2048]{2,0,1:T(8,128)S(1)} collective-permute-done((f32[32,4,2048]{2,0,1:T(8,128)S(1)}, f32[32,4,2048]{2,0,1:T(8,128)S(1)}, u32[]{:S(2)}, u32[]{:S(2)}) %collective-permute-start) | collective-permute-done | bytes 1048608 | tf_op jit(solution)/shard_map/ppermute | solution.py:20
  89.5 0.2 fusion.26
  89.6 0.0 copy-start.4
  89.7 1.2 %copy.33 = bf16[32,4,2048]{2,1,0:T(4,128)(2,1)} copy(bf16[32,4,2048]{2,0,1:T(8,128)(2,1)S(1)} %fusion.26) | data formatting | bytes 1048576 | tf_op jit(solution)/shard_map/convert_element_type | solution.py:130
  90.9 3.7 %all-to-all-start.2 = ((bf16[32,4,2048]{2,1,0:T(4,128)(2,1)}), bf16[32,4,2048]{2,1,0:T(4,128)(2,1)}, u32[]{:S(2)}, u32[]{:S(2)}) async-start(bf16[32,4,2048]{2,1,0:T(4,128)(2,1)} %copy.33), calls=%async_computation.3 | async-start | bytes 1048576 | tf_op jit(solution)/shard_map/all_to_all | solution.py:131
  94.6 0.1 convert_reduce_fusion
  94.8 0.1 convert_divide_fusion
  94.8 0.1 select_reduce_fusion
  94.9 15.3 %all-to-all-done.2 = bf16[32,4,2048]{2,1,0:T(4,128)(2,1)} async-done(((bf16[32,4,2048]{2,1,0:T(4,128)(2,1)}), bf16[32,4,2048]{2,1,0:T(4,128)(2,1)}, u32[]{:S(2)}, u32[]{:S(2)}) %all-to-all-start.2) | async-done | bytes 524320 | tf_op jit(solution)/shard_map/all_to_all | solution.py:131
  110.2 2.0 %reshape_reshape.4 = bf16[128,2048]{1,0:T(8,128)(2,1)} reshape(bf16[32,4,2048]{2,1,0:T(4,128)(2,1)} %all-to-all-done.2) | data formatting | bytes 1048576 | tf_op jit(solution)/shard_map/reshape;reshape | solution.py:135
  112.2 2.0 %convolution_convert_fusion.1 = bf16[8,2048]{1,0:T(8,128)(2,1)} fusion(f32[128,8]{0,1:T(8,128)S(1)} %select_reduce_fusion, bf16[128,2048]{1,0:T(8,128)(2,1)} %reshape_reshape.4), kind=kOutput, calls=%fused_computation.4 | convolution fusion | flops 25182208 | bytes 561152 | tf_op jit(solution)/shard_map/dot_general | solution.py:133
  (12 shorter events, 0.1 us)
Async XLA Ops:
  7.2 74.9 %copy-start = (bf16[1,2048,768]{2,1,0:T(8,128)(2,1)S(1)}, bf16[1,2048,768]{2,1,0:T(8,128)(2,1)}, u32[]{:S(2)}) copy-start(bf16[1,2048,768]{2,1,0:T(8,128)(2,1)} %param.20) | copy-start | bytes 9437188
  8.9 2.5 %copy-start.2 = (bf16[8,4096]{1,0:T(8,128)(2,1)S(1)}, bf16[8,4096]{1,0:T(8,128)(2,1)}, u32[]{:S(2)}) copy-start(bf16[8,4096]{1,0:T(8,128)(2,1)} %param.11) | copy-start | bytes 196612
  12.8 5.5 %copy-start.3 = (s32[8,8]{1,0:T(8,128)S(1)}, s32[8,8]{1,0:T(8,128)}, u32[]{:S(2)}) copy-start(s32[8,8]{1,0:T(8,128)} %param.18) | copy-start | bytes 772
  14.1 8.4 %all-to-all-start = ((bf16[4,8,1024]{2,1,0:T(8,128)(2,1)}), bf16[4,8,1024]{2,1,0:T(8,128)(2,1)S(1)}, u32[]{:S(2)}, u32[]{:S(2)}) async-start(bf16[4,8,1024]{2,1,0:T(8,128)(2,1)} %pad_maximum_fusion), calls=%async_computation | async-start | bytes 131072 | tf_op jit(solution)/shard_map/all_to_all | solution.py:88
  18.3 28.9 %reduce-scatter.2.cloned.1.call-start = ((), (), s32[]{:S(2)}) async-start(), calls=%async_computation.4 | async-start | bytes 327680 | tf_op jit(solution)/shard_map/reduce_scatter | solution.py:90
  18.4 28.8 %copy-start.1 = (bf16[8,2048]{1,0:T(8,128)(2,1)S(1)}, bf16[8,2048]{1,0:T(8,128)(2,1)}, u32[]{:S(2)}) copy-start(bf16[8,2048]{1,0:T(8,128)(2,1)} %param.15) | copy-start | bytes 98308
  18.4 30.4 %copy-start.5 = (f32[2048]{0:T(1024)S(1)}, f32[2048]{0:T(1024)}, u32[]{:S(2)}) copy-start(f32[2048]{0:T(1024)} %param.17) | copy-start | bytes 24580
  51.2 30.9 %all-to-all-start.1 = ((bf16[32,8,2048]{2,1,0:T(8,128)(2,1)}), bf16[32,8,2048]{2,1,0:T(8,128)(2,1)}, u32[]{:S(2)}, u32[]{:S(2)}) async-start(bf16[32,8,2048]{2,1,0:T(8,128)(2,1)} %bitcast.75), calls=%async_computation.2 | async-start | bytes 2097152 | tf_op jit(solution)/shard_map/all_to_all | solution.py:122
  86.7 2.7 %collective-permute-start = (f32[32,4,2048]{2,0,1:T(8,128)S(1)}, f32[32,4,2048]{2,0,1:T(8,128)S(1)}, u32[]{:S(2)}, u32[]{:S(2)}) collective-permute-start(f32[32,4,2048]{2,0,1:T(8,128)S(1)} %select_bitcast_fusion), channel_id=1, source_target_pairs={{0,1},{1,0},{2,3},{3,2},{4,5},{5,4},{6,7},{7,6},{8,9},{9,8},{10,11... | collective-permute-start | bytes 3145736 | tf_op jit(solution)/shard_map/ppermute | solution.py:20
  89.6 5.0 %copy-start.4 = (s32[8,8]{1,0:T(8,128)S(1)}, s32[8,8]{1,0:T(8,128)}, u32[]{:S(2)}) copy-start(s32[8,8]{1,0:T(8,128)} %param.19) | copy-start | bytes 772
  90.9 19.3 %all-to-all-start.2 = ((bf16[32,4,2048]{2,1,0:T(4,128)(2,1)}), bf16[32,4,2048]{2,1,0:T(4,128)(2,1)}, u32[]{:S(2)}, u32[]{:S(2)}) async-start(bf16[32,4,2048]{2,1,0:T(4,128)(2,1)} %copy.33), calls=%async_computation.3 | async-start | bytes 1048576 | tf_op jit(solution)/shard_map/all_to_all | solution.py:131
Sparse Core Ops, SparseCore 0:
  26.3 20.8 reduce-scatter.1
